TPU v7x, 32 devices: a whole 2x2x4 slice. The times are simulated.
32 devices in a mesh: row: 8 (over z, x), col: 4 (over y, core).
Axes of the slice: x: 2, y: 2, z: 4, core: 2. Of those that a mesh axis runs over, the one named last changes fastest.
Arguments:
- innovations: float32 [64, 16384], P(None, ('row', 'col')), may hold values from -300 to 300
- obs_factors: float32 [64, 16384], P(None, ('row', 'col')), may hold values from -6 to 6
- component: int32 [16384], P(('row', 'col')), may hold values 0 or 1
- obs_error: float32 [16384], P(('row', 'col')), may hold values from 0.5 to 2
- coupling: float32 [2, 2], replicated, may hold values from 0.5 to 2
- tile_slots: int32 [8, 4, 8, 3], P('row', 'col'), may hold values from 0 to 7, as said below
Outputs:
- increment: float32 [64, 16384], P(None, ('row', 'col'))
- residual: float32 [64, 16384], P(None, ('row', 'col'))
Inputs may be any that keep to these rules, and one draw needn't show every extreme that they name: `tile_slots`: each device's slots name distinct (local block row, local block column) pairs; on some device all 8 slots are live; the live flag is 0 or 1; local block rows are below 4 and local block columns below 8.
All inputs are finite; a program needn't handle non-finite values. No bound on the sum of `component` on one device may be relied on, other than what follows from the above.
Results may differ from a plain program's by a relative error of at most 0.0003.
Values sent between devices are 32-bit elements; how exact they have to be, the bound alone decides.
A program may use at most 64 MiB of HBM per device.

v0:
```python
import jax
import jax.numpy as jnp
from jax import lax
from jax.sharding import PartitionSpec as P

TILE = 512
ITERS = 3
length_sq = 12.0


def tile_matrix(left_factors, right_factors, left_labels, right_labels, coupling):
    left_norms = jnp.sum(left_factors * left_factors, axis=0)
    right_norms = jnp.sum(right_factors * right_factors, axis=0)
    products = lax.dot_general(
        left_factors,
        right_factors,
        (((0,), (0,)), ((), ())),
        precision=lax.Precision.HIGHEST,
        preferred_element_type=jnp.float32,
    )
    pair_coupling = (1.0 - left_labels)[:, None] * (
        (1.0 - right_labels)[None, :] * coupling[0, 0] + right_labels[None, :] * coupling[0, 1]
    ) + left_labels[:, None] * (
        (1.0 - right_labels)[None, :] * coupling[1, 0] + right_labels[None, :] * coupling[1, 1]
    )
    return pair_coupling * jnp.exp(
        -(left_norms[:, None] + right_norms[None, :] - 2.0 * products) / length_sq
    )


def take_segment(array, block):
    start = block * TILE
    return lax.dynamic_slice_in_dim(array, start, TILE, array.ndim - 1)


def add_segment(vector, block, values):
    start = block * TILE
    last_axis = vector.ndim - 1
    before = lax.dynamic_slice_in_dim(vector, start, TILE, last_axis)
    return lax.dynamic_update_slice_in_dim(vector, before + values, start, last_axis)


def squares(residual):
    return lax.psum(jnp.sum(residual * residual, axis=1), ("row", "col"))


def shards(innovations, obs_factors, component, obs_error, coupling, tile_slots):
    labels_float = component.astype(jnp.float32)
    row_factors, row_labels = (
        lax.all_gather(obs_factors, "col", axis=1, tiled=True),
        lax.all_gather(labels_float, "col", axis=0, tiled=True),
    )
    column_factors, column_labels = (
        lax.all_gather(obs_factors, "row", axis=1, tiled=True),
        lax.all_gather(labels_float, "row", axis=0, tiled=True),
    )
    slots = tile_slots[0, 0]
    count = slots.shape[0]
    flags = slots[:, 2].astype(jnp.float32)
    rhs_count = innovations.shape[0]

    def make_tile(number):
        row_block = slots[number, 0]
        column_block = slots[number, 1]
        block_matrix = tile_matrix(
            take_segment(row_factors, row_block),
            take_segment(column_factors, column_block),
            take_segment(row_labels, row_block),
            take_segment(column_labels, column_block),
            coupling,
        )
        return block_matrix * flags[number]

    def visit(totals, work):
        result = work(totals)
        return result

    stored = jnp.zeros((count, TILE, TILE), jnp.float32)

    def weigh(number, carry):

        def work(carry):
            row_totals, column_totals, stored = carry
            block_matrix = make_tile(number)
            row_totals = add_segment(row_totals, slots[number, 0], jnp.sum(block_matrix, axis=1))
            column_totals = add_segment(
                column_totals, slots[number, 1], jnp.sum(block_matrix, axis=0)
            )
            stored = lax.dynamic_update_index_in_dim(stored, block_matrix, number, 0)
            return (row_totals, column_totals, stored)

        return visit(carry, work)

    start_carry = (
        jnp.zeros((row_factors.shape[1],), jnp.float32),
        jnp.zeros((column_factors.shape[1],), jnp.float32),
        stored,
    )
    row_totals, column_totals, stored = lax.fori_loop(0, count, weigh, start_carry)
    diagonal = (
        obs_error
        + lax.psum_scatter(row_totals, "col", scatter_dimension=0, tiled=True)
        + lax.psum_scatter(column_totals, "row", scatter_dimension=0, tiled=True)
    )

    def fetch(number):
        block_matrix = lax.dynamic_index_in_dim(stored, number, 0, keepdims=False)
        return block_matrix

    increment = jnp.zeros_like(innovations)
    residual = innovations
    direction = innovations
    norm_now = squares(residual)
    for repeat in range(ITERS):
        column_values = lax.all_gather(direction, "row", axis=1, tiled=True)
        row_values = lax.all_gather(direction, "col", axis=1, tiled=True)

        def sweep(number, carry):

            def work(carry):
                row_image, column_image = carry
                block_matrix = fetch(number)
                row_block = slots[number, 0]
                column_block = slots[number, 1]
                right_part = lax.dot_general(
                    take_segment(column_values, column_block),
                    block_matrix,
                    (((1,), (1,)), ((), ())),
                    precision=lax.Precision.HIGHEST,
                    preferred_element_type=jnp.float32,
                )
                left_part = jnp.dot(
                    take_segment(row_values, row_block),
                    block_matrix,
                    precision=lax.Precision.HIGHEST,
                    preferred_element_type=jnp.float32,
                )
                return (
                    add_segment(row_image, row_block, right_part),
                    add_segment(column_image, column_block, left_part),
                )

            return visit(carry, work)

        start_image = (
            jnp.zeros((rhs_count, row_values.shape[1]), jnp.float32),
            jnp.zeros((rhs_count, column_values.shape[1]), jnp.float32),
        )
        row_image, column_image = lax.fori_loop(0, count, sweep, start_image)
        image = (
            diagonal[None, :] * direction
            + lax.psum_scatter(row_image, "col", scatter_dimension=1, tiled=True)
            + lax.psum_scatter(column_image, "row", scatter_dimension=1, tiled=True)
        )
        alpha = norm_now / lax.psum(jnp.sum(direction * image, axis=1), ("row", "col"))
        increment = increment + alpha[:, None] * direction
        residual = residual - alpha[:, None] * image
        norm_next = squares(residual)
        direction = residual + (norm_next / norm_now)[:, None] * direction
        norm_now = norm_next
    return (increment, residual)


def solution(mesh):
    return jax.shard_map(
        shards,
        mesh=mesh,
        in_specs=(
            P(None, ("row", "col")),
            P(None, ("row", "col")),
            P(("row", "col")),
            P(("row", "col")),
            P(),
            P("row", "col", None, None),
        ),
        out_specs=(P(None, ("row", "col")), P(None, ("row", "col"))),
        check_vma=False,
    )
```

profile of v0, /device:TPU:0, one launch (start us, length us, event | category | flops | bytes accessed | tf_op | source)
XLA Modules:
  0.0 869.6 jit_solution(11168833523570514415)
XLA Ops:
  9.4 28.0 %all-gather.1 = f32[8,1,512]{2,1,0:T(1,128)S(1)} all-gather(f32[1,1,512]{2,1,0:T(1,128)S(1)} %bitcast.84), channel_id=1, replica_groups=mesh['row'=8,'col'=4] {'row'}, dimensions={0}, use_global_device_ids=true | all-gather | bytes 18432 | tf_op jit(solution)/shard_map/all_gather | solution.py:55
  37.4 5.2 all-gather
  42.6 7.5 all_gather.32
  50.0 7.5 all_gather.35
  58.2 95.6 %while.62 = (s32[]{:T(128)}, f32[2048]{0:T(1024)S(1)}, f32[4096]{0:T(1024)S(1)}, f32[8,512,512]{2,1,0:T(8,128)}, s32[8,3]{0,1:T(4,128)S(1)}, /*index=5*/f32[2048...) while((s32[]{:T(128)}, f32[2048]{0:T(1024)S(1)}, ...), condition=%wide.region_7.8_spmd, body=%wide.region_2.7_spmd.sunk | while | flops 204606480 | bytes 3716449 | solution.py:99
  65.8 3.0 fusion.62
  77.7 3.1 fusion.62
  89.7 3.0 fusion.62
  101.7 3.0 fusion.62
  113.6 3.0 fusion.62
  125.5 3.0 fusion.62
  137.5 3.0 fusion.62
  149.5 3.0 fusion.62
  154.0 50.7 %while.63 = (s32[]{:T(128)}, f32[64,2048]{1,0:T(8,128)S(1)}, f32[64,4096]{1,0:T(8,128)S(1)}, s32[8,3]{0,1:T(4,128)S(1)}, f32[64,4096]{1,0:T(8,128)}, /*index=5*/...) while((s32[]{:T(128)}, f32[64,2048]{1,0:T(8,128)S(1)}, ...), condition=%wide.region_11.12_spmd, body=%wide.region_10.11_spmd.sunk | while | flops 402718720 | bytes 2884853 | solution.py:149
  208.7 35.7 %all-reduce.1 = f32[4096]{0:T(1024)S(1)} all-reduce(f32[4096]{0:T(1024)S(1)} %get-tuple-element.564), channel_id=3, replica_groups=mesh['row'=8,'col'=4] {'row'}, use_global_device_ids=true, to_apply=%region_9.10.clone | all-reduce | flops 4096 | bytes 32768
  244.3 6.1 all-reduce
  250.6 44.0 %reduce-scatter.9.cloned.1.call-done = f32[64,512]{1,0:T(8,128)} async-done(((f32[64,4096]{1,0:T(8,128)}), f32[64,512]{1,0:T(8,128)}) %reduce-scatter.9.cloned.1.call-update) | async-done | bytes 131088 | tf_op jit(solution)/shard_map/reduce_scatter | solution.py:153
  295.7 39.8 %all-reduce.2 = (f32[64]{0:T(128)S(1)}, f32[64]{0:T(128)S(1)}) all-reduce(f32[64]{0:T(128)S(1)} %get-tuple-element.575, f32[64]{0:T(128)S(1)} %get-tuple-element.574), channel_id=1, replica_groups=mesh['row'=8,'col'=4] {'row','col'}, use_global_device_ids=true, to_apply=%region_1.2 | all-reduce | flops 128 | bytes 1024 | tf_op jit(solution)/shard_map/psum | solution.py:44
  336.7 39.3 %psum.44 = f32[64]{0:T(128)S(1)} all-reduce(f32[64]{0:T(128)S(1)} %get-tuple-element.646), channel_id=1, replica_groups=mesh['row'=8,'col'=4] {'row','col'}, use_global_device_ids=true, to_apply=%region_17.18 | all-reduce | flops 64 | bytes 512 | tf_op jit(solution)/shard_map/psum | solution.py:44
  376.8 8.2 all_gather.37
  384.9 32.0 %all-gather.11.cloned.1.call-done = f32[64,4096]{1,0:T(8,128)} async-done(((f32[64,512]{1,0:T(8,128)}), f32[64,4096]{1,0:T(8,128)}) %all-gather.11.cloned.1.call-update) | async-done | bytes 1048592 | tf_op jit(solution)/shard_map/all_gather | solution.py:115
  417.1 51.1 %while.64 = (s32[]{:T(128)}, f32[64,2048]{1,0:T(8,128)S(1)}, f32[64,4096]{1,0:T(8,128)S(1)}, s32[8,3]{0,1:T(4,128)S(1)}, f32[64,4096]{1,0:T(8,128)}, /*index=5*/...) while((s32[]{:T(128)}, f32[64,2048]{1,0:T(8,128)S(1)}, ...), condition=%wide.region_19.20_spmd, body=%wide.region_18.19_spmd.sunk | while | flops 402718720 | bytes 2884853 | solution.py:149
  469.8 19.7 %reduce-scatter.11.cloned.1.call-done = f32[64,512]{1,0:T(8,128)} async-done(((f32[64,2048]{1,0:T(8,128)}), f32[64,512]{1,0:T(8,128)}) %reduce-scatter.11.cloned.1.call-update) | async-done | bytes 131088 | tf_op jit(solution)/shard_map/reduce_scatter | solution.py:152
  489.5 68.0 %reduce-scatter.13.cloned.1.call-done = f32[64,512]{1,0:T(8,128)} async-done(((f32[64,4096]{1,0:T(8,128)}), f32[64,512]{1,0:T(8,128)}) %reduce-scatter.13.cloned.1.call-update) | async-done | bytes 131088 | tf_op jit(solution)/shard_map/reduce_scatter | solution.py:153
  558.6 39.9 %psum.45 = f32[64]{0:T(128)S(1)} all-reduce(f32[64]{0:T(128)S(1)} %multiply_reduce_fusion.4), channel_id=1, replica_groups=mesh['row'=8,'col'=4] {'row','col'}, use_global_device_ids=true, to_apply=%region_23.24 | all-reduce | flops 64 | bytes 512 | tf_op jit(solution)/shard_map/psum | solution.py:155
  599.7 39.3 %psum.46 = f32[64]{0:T(128)S(1)} all-reduce(f32[64]{0:T(128)S(1)} %get-tuple-element.644), channel_id=1, replica_groups=mesh['row'=8,'col'=4] {'row','col'}, use_global_device_ids=true, to_apply=%region_25.26 | all-reduce | flops 64 | bytes 512 | tf_op jit(solution)/shard_map/psum | solution.py:44
  639.7 8.3 all_gather.39
  648.1 31.8 %all-gather.13.cloned.1.call-done = f32[64,4096]{1,0:T(8,128)} async-done(((f32[64,512]{1,0:T(8,128)}), f32[64,4096]{1,0:T(8,128)}) %all-gather.13.cloned.1.call-update) | async-done | bytes 1048592 | tf_op jit(solution)/shard_map/all_gather | solution.py:115
  680.0 51.1 %while.65 = (s32[]{:T(128)}, f32[64,2048]{1,0:T(8,128)S(1)}, f32[64,4096]{1,0:T(8,128)S(1)}, s32[8,3]{0,1:T(4,128)S(1)}, f32[64,4096]{1,0:T(8,128)}, /*index=5*/...) while((s32[]{:T(128)}, f32[64,2048]{1,0:T(8,128)S(1)}, ...), condition=%wide.region_27.28_spmd, body=%wide.region_26.27_spmd.sunk | while | flops 402718720 | bytes 2884853 | solution.py:149
  732.5 19.9 %reduce-scatter.15.cloned.1.call-done = f32[64,512]{1,0:T(8,128)} async-done(((f32[64,2048]{1,0:T(8,128)}), f32[64,512]{1,0:T(8,128)}) %reduce-scatter.15.cloned.1.call-update) | async-done | bytes 131088 | tf_op jit(solution)/shard_map/reduce_scatter | solution.py:152
  752.4 67.6 %reduce-scatter.17.cloned.1.call-done = f32[64,512]{1,0:T(8,128)} async-done(((f32[64,4096]{1,0:T(8,128)}), f32[64,512]{1,0:T(8,128)}) %reduce-scatter.17.cloned.1.call-update) | async-done | bytes 131088 | tf_op jit(solution)/shard_map/reduce_scatter | solution.py:153
  821.1 39.9 %psum.47 = f32[64]{0:T(128)S(1)} all-reduce(f32[64]{0:T(128)S(1)} %multiply_reduce_fusion.2), channel_id=1, replica_groups=mesh['row'=8,'col'=4] {'row','col'}, use_global_device_ids=true, to_apply=%region_31.32 | all-reduce | flops 64 | bytes 512 | tf_op jit(solution)/shard_map/psum | solution.py:155
  (211 shorter events, 200.4 us)
Async XLA Ops:
  7.2 51.0 %all-gather.7.cloned.1.call-start = ((), (), s32[]{:S(2)}) async-start(), calls=%async_computation.6 | async-start | bytes 1179648 | tf_op jit(solution)/shard_map/all_gather | solution.py:54
  7.9 146.0 %all-gather.9.cloned.1.call-start = ((), (), s32[]{:S(2)}) async-start(), calls=%async_computation.7 | async-start | bytes 1179648 | tf_op jit(solution)/shard_map/all_gather | solution.py:115
  8.6 241.9 %reduce-scatter.7.cloned.1.call-start = ((), (), s32[]{:S(2)}) async-start(), calls=%async_computation.8 | async-start | bytes 655360 | tf_op jit(solution)/shard_map/reduce_scatter | solution.py:152
  153.9 52.3 %copy-start.11 = (u32[32]{0:T(128)S(1)}, u32[32]{0:T(128)}, u32[]{:S(2)}) copy-start(u32[32]{0:T(128)} %constant.217) | copy-start | bytes 388
  154.0 52.8 %copy-start.10 = (u32[32]{0:T(128)S(1)}, u32[32]{0:T(128)}, u32[]{:S(2)}) copy-start(u32[32]{0:T(128)} %constant.221) | copy-start | bytes 388
  154.0 96.5 %copy-start.9 = (f32[512]{0:T(512)S(1)}, f32[512]{0:T(512)}, u32[]{:S(2)}) copy-start(f32[512]{0:T(512)} %param.17) | copy-start | bytes 6148
  154.0 140.6 %copy-start.7 = (f32[64,512]{1,0:T(8,128)S(1)}, f32[64,512]{1,0:T(8,128)}, u32[]{:S(2)}) copy-start(f32[64,512]{1,0:T(8,128)} %param.14) | copy-start | bytes 393220
  204.7 0.8 copy-start.5
  204.8 1.2 copy-start.1
  205.6 89.0 %reduce-scatter.9.cloned.1.call-start = ((), (), s32[]{:S(2)}) async-start(), calls=%async_computation.9 | async-start | bytes 1179648 | tf_op jit(solution)/shard_map/reduce_scatter | solution.py:153
  206.1 210.8 %all-gather.11.cloned.1.call-start = ((), (), s32[]{:S(2)}) async-start(), calls=%async_computation.10 | async-start | bytes 1179648 | tf_op jit(solution)/shard_map/all_gather | solution.py:115
  376.7 112.8 %reduce-scatter.11.cloned.1.call-start = ((), (), s32[]{:S(2)}) async-start(), calls=%async_computation.11 | async-start | bytes 655360 | tf_op jit(solution)/shard_map/reduce_scatter | solution.py:152
  417.0 140.5 %copy-start.3 = (f32[64,512]{1,0:T(8,128)S(1)}, f32[64,512]{1,0:T(8,128)}, u32[]{:S(2)}) copy-start(f32[64,512]{1,0:T(8,128)} %multiply_add_fusion.4) | copy-start | bytes 393220
  468.2 0.8 copy-start.6
  468.2 1.2 copy-start.2
  469.0 88.5 %reduce-scatter.13.cloned.1.call-start = ((), (), s32[]{:S(2)}) async-start(), calls=%async_computation.12 | async-start | bytes 1179648 | tf_op jit(solution)/shard_map/reduce_scatter | solution.py:153
  469.8 210.1 %all-gather.13.cloned.1.call-start = ((), (), s32[]{:S(2)}) async-start(), calls=%async_computation.13 | async-start | bytes 1179648 | tf_op jit(solution)/shard_map/all_gather | solution.py:115
  639.7 112.7 %reduce-scatter.15.cloned.1.call-start = ((), (), s32[]{:S(2)}) async-start(), calls=%async_computation.14 | async-start | bytes 655360 | tf_op jit(solution)/shard_map/reduce_scatter | solution.py:152
  679.9 140.1 %copy-start.8 = (f32[64,512]{1,0:T(8,128)S(1)}, f32[64,512]{1,0:T(8,128)}, u32[]{:S(2)}) copy-start(f32[64,512]{1,0:T(8,128)} %multiply_add_fusion.3) | copy-start | bytes 393220
  731.1 0.8 copy-start.4
  731.1 1.2 copy-start
  731.9 88.1 %reduce-scatter.17.cloned.1.call-start = ((), (), s32[]{:S(2)}) async-start(), calls=%async_computation.15 | async-start | bytes 1179648 | tf_op jit(solution)/shard_map/reduce_scatter | solution.py:153
Sparse Core Ops, SparseCore 0:
  10.2 42.9 all-gather.6
  55.3 38.9 all-gather.8
  205.7 20.9 reduce-scatter.6
  230.0 64.5 reduce-scatter.8
  376.9 40.0 all-gather.10
  469.1 20.3 reduce-scatter.10
  492.9 64.5 reduce-scatter.12
  639.8 40.0 all-gather.12
  732.1 20.3 reduce-scatter.14
  755.7 64.2 reduce-scatter.16
where the time goes:
time: 873 us; the launch traced here: 870 us
  blocking collectives  305 us (35%)
  waiting for transfers between devices  285 us (33%)
  matrix products  130 us (15%)
  local copies, waits for them, and re-layouts  52 us (6%)
  loops' own time  41.6 us (5%)
  other arithmetic  40.3 us (5%)
  between operations  15.7 us (2%)
    reduce_scatter x3, waiting for transfers between devices, shards(): lax.psum_scatter(column_image, 'row', scatter_dimension=1, tiled=True)  180 us
    psum x3, blocking collectives, squares(): return lax.psum(jnp.sum(residual * residual, axis=1), ('row', 'col'))  118 us
    psum x2, blocking collectives, shards(): lax.psum(jnp.sum(direction * image, axis=1), ('row', 'col'))  79.7 us
    all_gather x3, waiting for transfers between devices, shards(): column_values = lax.all_gather(direction, 'row', axis=1, tiled=True)  63.8 us
    dot_general x24, matrix products, work(): lax.dot_general(take_segment(column_values, column_block), block_matrix,...  58.1 us
    dot_general x24, matrix products, work(): jnp.dot(take_segment(row_values, row_block), block_matrix, precision=lax....  47.4 us
    unnamed x2, blocking collectives  41.8 us
    reduce_scatter x3, waiting for transfers between devices, shards(): lax.psum_scatter(row_image, 'col', scatter_dimension=1, tiled=True)  39.6 us
  transfers between devices with their start and end apart: 10, of which 7 were waited for; matrix products, arithmetic and copies ran while one was open for 10% of the time, Pallas kernels for 0%

commit v1 on v0

--- a/solution.py
+++ b/solution.py
@@ -112,7 +112,7 @@
     direction = innovations
     norm_now = squares(residual)
     for repeat in range(ITERS):
-        column_values = lax.all_gather(direction, "row", axis=1, tiled=True)
+        column_values = jnp.concatenate(lax.all_gather(direction, "row"), axis=1)
         row_values = lax.all_gather(direction, "col", axis=1, tiled=True)
 
         def sweep(number, carry):

time: 873 us -> 874 us (level)
  no operation moved by 1% of the time
where the time goes in v1:
time: 874 us; the launch traced here: 870 us
  blocking collectives  305 us (35%)
  waiting for transfers between devices  285 us (33%)
  matrix products  128 us (15%)
  local copies, waits for them, and re-layouts  54.6 us (6%)
  other arithmetic  42.4 us (5%)
  loops' own time  39.5 us (5%)
  between operations  15.7 us (2%)
    reduce_scatter x3, waiting for transfers between devices, shards(): lax.psum_scatter(column_image, 'row', scatter_dimension=1, tiled=True)  179 us
    psum x3, blocking collectives, squares(): return lax.psum(jnp.sum(residual * residual, axis=1), ('row', 'col'))  118 us
    psum x2, blocking collectives, shards(): lax.psum(jnp.sum(direction * image, axis=1), ('row', 'col'))  79.7 us
    all_gather x3, waiting for transfers between devices, shards(): column_values = jnp.concatenate(lax.all_gather(direction, 'row'), axis=1)  63.9 us
    dot_general x24, matrix products, work(): lax.dot_general(take_segment(column_values, column_block), block_matrix,...  56.2 us
    dot_general x24, matrix products, work(): jnp.dot(take_segment(row_values, row_block), block_matrix, precision=lax....  47.4 us
    unnamed x2, blocking collectives  41.8 us
    reduce_scatter x3, waiting for transfers between devices, shards(): lax.psum_scatter(row_image, 'col', scatter_dimension=1, tiled=True)  39.7 us
  transfers between devices with their start and end apart: 10, of which 7 were waited for; matrix products, arithmetic and copies ran while one was open for 10% of the time, Pallas kernels for 0%

profile of v1, /device:TPU:0, one launch (start us, length us, event | category | flops | bytes accessed | tf_op | source)
XLA Modules:
  0.0 870.1 jit_solution(1445822795249530354)
XLA Ops:
  9.4 28.0 %all-gather.4 = f32[8,1,512]{2,1,0:T(1,128)S(1)} all-gather(f32[1,1,512]{2,1,0:T(1,128)S(1)} %bitcast.106), channel_id=1, replica_groups=mesh['row'=8,'col'=4] {'row'}, dimensions={0}, use_global_device_ids=true | all-gather | bytes 18432 | tf_op jit(solution)/shard_map/all_gather | solution.py:55
  37.4 5.2 all-gather.3
  42.6 7.5 all_gather.41
  50.0 7.5 all_gather.45
  58.2 95.6 %while.62 = (s32[]{:T(128)}, f32[2048]{0:T(1024)S(1)}, f32[4096]{0:T(1024)S(1)}, f32[8,512,512]{2,1,0:T(8,128)}, s32[8,3]{0,1:T(4,128)S(1)}, /*index=5*/f32[2048...) while((s32[]{:T(128)}, f32[2048]{0:T(1024)S(1)}, ...), condition=%wide.region_7.8_spmd, body=%wide.region_2.7_spmd.sunk | while | flops 204606480 | bytes 3716449 | solution.py:99
  65.8 3.0 fusion.62
  77.7 3.1 fusion.62
  89.7 3.0 fusion.62
  101.7 3.0 fusion.62
  113.6 3.0 fusion.62
  125.5 3.0 fusion.62
  137.5 3.0 fusion.62
  149.5 3.0 fusion.62
  155.4 49.2 %while.63 = (s32[]{:T(128)}, f32[64,2048]{1,0:T(8,128)S(1)}, f32[64,4096]{1,0:T(8,128)S(1)}, s32[8,3]{0,1:T(4,128)S(1)}, f32[64,4096]{1,0:T(8,128)S(1)}, /*index...) while((s32[]{:T(128)}, f32[64,2048]{1,0:T(8,128)S(1)}, ...), condition=%wide.region_11.12_spmd, body=%wide.region_10.11_spmd.sunk | while | flops 402718720 | bytes 2884853 | solution.py:149
  208.5 35.6 %all-reduce.1 = f32[4096]{0:T(1024)S(1)} all-reduce(f32[4096]{0:T(1024)S(1)} %get-tuple-element.564), channel_id=6, replica_groups=mesh['row'=8,'col'=4] {'row'}, use_global_device_ids=true, to_apply=%region_9.10.clone | all-reduce | flops 4096 | bytes 32768
  244.1 6.1 all-reduce
  250.4 43.9 %reduce-scatter.9.cloned.1.call-done = f32[64,512]{1,0:T(8,128)} async-done(((f32[64,4096]{1,0:T(8,128)}), f32[64,512]{1,0:T(8,128)}) %reduce-scatter.9.cloned.1.call-update) | async-done | bytes 131088 | tf_op jit(solution)/shard_map/reduce_scatter | solution.py:153
  295.4 39.8 %all-reduce.2 = (f32[64]{0:T(128)S(1)}, f32[64]{0:T(128)S(1)}) all-reduce(f32[64]{0:T(128)S(1)} %get-tuple-element.575, f32[64]{0:T(128)S(1)} %get-tuple-element.574), channel_id=1, replica_groups=mesh['row'=8,'col'=4] {'row','col'}, use_global_device_ids=true, to_apply=%region_1.2 | all-reduce | flops 128 | bytes 1024 | tf_op jit(solution)/shard_map/psum | solution.py:44
  336.4 39.3 %psum.44 = f32[64]{0:T(128)S(1)} all-reduce(f32[64]{0:T(128)S(1)} %get-tuple-element.646), channel_id=1, replica_groups=mesh['row'=8,'col'=4] {'row','col'}, use_global_device_ids=true, to_apply=%region_17.18 | all-reduce | flops 64 | bytes 512 | tf_op jit(solution)/shard_map/psum | solution.py:44
  376.5 8.2 all_gather.48
  384.7 32.0 %all-gather.14.cloned.1.call-done = f32[512,512]{1,0:T(8,128)} async-done(((f32[64,512]{1,0:T(8,128)}), f32[512,512]{1,0:T(8,128)}) %all-gather.14.cloned.1.call-update) | async-done | bytes 1048592 | tf_op jit(solution)/shard_map/all_gather | solution.py:115
  418.1 49.1 %while.64 = (s32[]{:T(128)}, f32[64,2048]{1,0:T(8,128)S(1)}, f32[64,4096]{1,0:T(8,128)S(1)}, s32[8,3]{0,1:T(4,128)S(1)}, f32[64,4096]{1,0:T(8,128)S(1)}, /*index...) while((s32[]{:T(128)}, f32[64,2048]{1,0:T(8,128)S(1)}, ...), condition=%wide.region_19.20_spmd, body=%wide.region_18.19_spmd.sunk | while | flops 402718720 | bytes 2884853 | solution.py:149
  468.9 19.7 %reduce-scatter.11.cloned.1.call-done = f32[64,512]{1,0:T(8,128)} async-done(((f32[64,2048]{1,0:T(8,128)}), f32[64,512]{1,0:T(8,128)}) %reduce-scatter.11.cloned.1.call-update) | async-done | bytes 131088 | tf_op jit(solution)/shard_map/reduce_scatter | solution.py:152
  488.6 68.0 %reduce-scatter.13.cloned.1.call-done = f32[64,512]{1,0:T(8,128)} async-done(((f32[64,4096]{1,0:T(8,128)}), f32[64,512]{1,0:T(8,128)}) %reduce-scatter.13.cloned.1.call-update) | async-done | bytes 131088 | tf_op jit(solution)/shard_map/reduce_scatter | solution.py:153
  557.7 39.9 %psum.45 = f32[64]{0:T(128)S(1)} all-reduce(f32[64]{0:T(128)S(1)} %multiply_reduce_fusion.4), channel_id=1, replica_groups=mesh['row'=8,'col'=4] {'row','col'}, use_global_device_ids=true, to_apply=%region_23.24 | all-reduce | flops 64 | bytes 512 | tf_op jit(solution)/shard_map/psum | solution.py:155
  599.4 39.2 %psum.46 = f32[64]{0:T(128)S(1)} all-reduce(f32[64]{0:T(128)S(1)} %get-tuple-element.644), channel_id=1, replica_groups=mesh['row'=8,'col'=4] {'row','col'}, use_global_device_ids=true, to_apply=%region_25.26 | all-reduce | flops 64 | bytes 512 | tf_op jit(solution)/shard_map/psum | solution.py:44
  640.2 8.3 all_gather.51
  648.5 31.8 %all-gather.16.cloned.1.call-done = f32[512,512]{1,0:T(8,128)} async-done(((f32[64,512]{1,0:T(8,128)}), f32[512,512]{1,0:T(8,128)}) %all-gather.16.cloned.1.call-update) | async-done | bytes 1048592 | tf_op jit(solution)/shard_map/all_gather | solution.py:115
  681.8 49.1 %while.65 = (s32[]{:T(128)}, f32[64,2048]{1,0:T(8,128)S(1)}, f32[64,4096]{1,0:T(8,128)S(1)}, s32[8,3]{0,1:T(4,128)S(1)}, f32[64,4096]{1,0:T(8,128)S(1)}, /*index...) while((s32[]{:T(128)}, f32[64,2048]{1,0:T(8,128)S(1)}, ...), condition=%wide.region_27.28_spmd, body=%wide.region_26.27_spmd.sunk | while | flops 402718720 | bytes 2884853 | solution.py:149
  732.4 19.9 %reduce-scatter.15.cloned.1.call-done = f32[64,512]{1,0:T(8,128)} async-done(((f32[64,2048]{1,0:T(8,128)}), f32[64,512]{1,0:T(8,128)}) %reduce-scatter.15.cloned.1.call-update) | async-done | bytes 131088 | tf_op jit(solution)/shard_map/reduce_scatter | solution.py:152
  752.3 67.4 %reduce-scatter.17.cloned.1.call-done = f32[64,512]{1,0:T(8,128)} async-done(((f32[64,4096]{1,0:T(8,128)}), f32[64,512]{1,0:T(8,128)}) %reduce-scatter.17.cloned.1.call-update) | async-done | bytes 131088 | tf_op jit(solution)/shard_map/reduce_scatter | solution.py:153
  820.9 39.9 %psum.47 = f32[64]{0:T(128)S(1)} all-reduce(f32[64]{0:T(128)S(1)} %multiply_reduce_fusion.2), channel_id=1, replica_groups=mesh['row'=8,'col'=4] {'row','col'}, use_global_device_ids=true, to_apply=%region_31.32 | all-reduce | flops 64 | bytes 512 | tf_op jit(solution)/shard_map/psum | solution.py:155
  (220 shorter events, 203.1 us)
Async XLA Ops:
  7.2 51.0 %all-gather.10.cloned.1.call-start = ((), (), s32[]{:S(2)}) async-start(), calls=%async_computation.6 | async-start | bytes 1179648 | tf_op jit(solution)/shard_map/all_gather | solution.py:54
  7.9 146.0 %all-gather.12.cloned.1.call-start = ((), (), s32[]{:S(2)}) async-start(), calls=%async_computation.13 | async-start | bytes 1179648 | tf_op jit(solution)/shard_map/all_gather | solution.py:115
  8.6 241.7 %reduce-scatter.7.cloned.1.call-start = ((), (), s32[]{:S(2)}) async-start(), calls=%async_computation.7 | async-start | bytes 655360 | tf_op jit(solution)/shard_map/reduce_scatter | solution.py:152
  155.3 50.8 %copy-start.12 = (u32[32]{0:T(128)S(1)}, u32[32]{0:T(128)}, u32[]{:S(2)}) copy-start(u32[32]{0:T(128)} %constant.217) | copy-start | bytes 388
  155.3 51.3 %copy-start.11 = (u32[32]{0:T(128)S(1)}, u32[32]{0:T(128)}, u32[]{:S(2)}) copy-start(u32[32]{0:T(128)} %constant.221) | copy-start | bytes 388
  155.3 95.0 %copy-start.10 = (f32[512]{0:T(512)S(1)}, f32[512]{0:T(512)}, u32[]{:S(2)}) copy-start(f32[512]{0:T(512)} %param.17) | copy-start | bytes 6148
  155.3 139.0 %copy-start.7 = (f32[64,512]{1,0:T(8,128)S(1)}, f32[64,512]{1,0:T(8,128)}, u32[]{:S(2)}) copy-start(f32[64,512]{1,0:T(8,128)} %param.14) | copy-start | bytes 393220
  204.6 0.8 copy-start.5
  204.6 1.2 copy-start.1
  205.4 88.9 %reduce-scatter.9.cloned.1.call-start = ((), (), s32[]{:S(2)}) async-start(), calls=%async_computation.8 | async-start | bytes 1179648 | tf_op jit(solution)/shard_map/reduce_scatter | solution.py:153
  206.0 210.7 %all-gather.14.cloned.1.call-start = ((), (), s32[]{:S(2)}) async-start(), calls=%async_computation.14 | async-start | bytes 1179648 | tf_op jit(solution)/shard_map/all_gather | solution.py:115
  375.7 42.3 %copy-start.13 = (f32[64]{0:T(128)}, f32[64]{0:T(128)S(1)}, u32[]{:S(2)}) copy-start(f32[64]{0:T(128)S(1)} %psum.44) | copy-start | bytes 772
  376.5 112.1 %reduce-scatter.11.cloned.1.call-start = ((), (), s32[]{:S(2)}) async-start(), calls=%async_computation.9 | async-start | bytes 655360 | tf_op jit(solution)/shard_map/reduce_scatter | solution.py:152
  418.1 138.5 %copy-start.3 = (f32[64,512]{1,0:T(8,128)S(1)}, f32[64,512]{1,0:T(8,128)}, u32[]{:S(2)}) copy-start(f32[64,512]{1,0:T(8,128)} %multiply_add_fusion.4) | copy-start | bytes 393220
  467.3 0.8 copy-start.6
  467.3 1.2 copy-start.2
  468.1 88.5 %reduce-scatter.13.cloned.1.call-start = ((), (), s32[]{:S(2)}) async-start(), calls=%async_computation.10 | async-start | bytes 1179648 | tf_op jit(solution)/shard_map/reduce_scatter | solution.py:153
  468.8 211.5 %all-gather.16.cloned.1.call-start = ((), (), s32[]{:S(2)}) async-start(), calls=%async_computation.15 | async-start | bytes 1179648 | tf_op jit(solution)/shard_map/all_gather | solution.py:115
  599.4 82.3 %copy-start.9 = (f32[64,512]{1,0:T(8,128)}, f32[64,512]{1,0:T(8,128)S(1)}, u32[]{:S(2)}) copy-start(f32[64,512]{1,0:T(8,128)S(1)} %get-tuple-element.645) | copy-start | bytes 393220
  638.7 43.0 %copy-start.14 = (f32[64]{0:T(128)}, f32[64]{0:T(128)S(1)}, u32[]{:S(2)}) copy-start(f32[64]{0:T(128)S(1)} %psum.46) | copy-start | bytes 772
  640.1 112.2 %reduce-scatter.15.cloned.1.call-start = ((), (), s32[]{:S(2)}) async-start(), calls=%async_computation.11 | async-start | bytes 655360 | tf_op jit(solution)/shard_map/reduce_scatter | solution.py:152
  681.8 138.0 %copy-start.8 = (f32[64,512]{1,0:T(8,128)S(1)}, f32[64,512]{1,0:T(8,128)}, u32[]{:S(2)}) copy-start(f32[64,512]{1,0:T(8,128)} %multiply_add_fusion.3) | copy-start | bytes 393220
  731.0 0.8 copy-start.4
  731.0 1.2 copy-start
  731.8 88.0 %reduce-scatter.17.cloned.1.call-start = ((), (), s32[]{:S(2)}) async-start(), calls=%async_computation.12 | async-start | bytes 1179648 | tf_op jit(solution)/shard_map/reduce_scatter | solution.py:153
Sparse Core Ops, SparseCore 0:
  10.2 42.9 all-gather.9
  55.3 39.1 all-gather.11
  205.5 20.9 reduce-scatter.6
  229.8 64.4 reduce-scatter.8
  376.6 40.0 all-gather.13
  468.2 20.3 reduce-scatter.10
  492.0 64.5 reduce-scatter.12
  640.2 40.0 all-gather.15
  731.9 20.3 reduce-scatter.14
  755.6 64.1 reduce-scatter.16
